TPU v7x, 512 devices: a whole 4x4x16 slice. The times are simulated.
512 devices in a mesh: section: 16 (over z), expert: 8 (over y, core), dp: 4 (over x).
Axes of the slice: x: 4, y: 4, z: 16, core: 2. Of those that a mesh axis runs over, the one named last changes fastest.
Arguments:
- tokens: bfloat16 [1024, 3072], P('expert', 'dp'), may hold values from -6 to 6
- expert_ids: int32 [1024, 2], P('expert'), may hold values from 0 to 7, all different within a row; in each aligned block of 128 rows (0 to 127, 128 to 255, ...) at most 64 rows name the same one
- w_gate: bfloat16 [8, 3072, 8192], P('expert', 'dp', 'section'), may hold values from -0.109375 to 0.109375
- w_up: bfloat16 [8, 3072, 8192], P('expert', 'dp', 'section'), may hold values from -0.109375 to 0.109375
- cotangent: bfloat16 [8, 512, 8192], P('expert', None, 'section'), may hold values from -6 to 6
Outputs:
- acted: bfloat16 [8, 512, 8192], P('expert', None, 'section')
- input_grad: bfloat16 [1024, 3072], P('expert', 'dp')
- gate_grad: bfloat16 [8, 3072, 8192], P('expert', 'dp', 'section')
- up_grad: bfloat16 [8, 3072, 8192], P('expert', 'dp', 'section')
Inputs may be any that keep to these rules, and one draw needn't show every extreme that they name: `expert_ids`: each token names two different experts. Among the 128 tokens of one index of the expert axis no expert is named more than 64 times, a bound that some block reaches.
All inputs are finite; a program needn't handle non-finite values.
Results may differ from a plain program's by a relative error of at most 0.0049.
Values may be sent and summed in bfloat16 or wider, within the bound.
A program may use at most 64 MiB of HBM per device.

v0:
```python
import jax
import jax.numpy as jnp
from jax import lax
from jax.sharding import PartitionSpec as P


def local(tokens, expert_ids, w_gate, w_up, cotangent):
    rows, width = tokens.shape
    experts = lax.axis_size("expert")
    capacity = min(rows, 4 * rows // experts)
    wg = w_gate[0]
    wu = w_up[0]
    flat_ids = expert_ids.reshape(-1)
    member = (flat_ids[:, None] == jnp.arange(experts, dtype=jnp.int32)[None, :]).astype(jnp.int32)
    rank = jnp.sum((jnp.cumsum(member, axis=0) - member) * member, axis=1)
    slot = flat_ids * capacity + rank
    token_of = jnp.arange(2 * rows, dtype=jnp.int32) // 2
    source = jnp.full((experts * capacity,), rows, jnp.int32).at[slot].set(token_of)
    occupied = jnp.zeros((experts * capacity,), jnp.bfloat16).at[slot].set(1.0)
    x_pad = jnp.concatenate([tokens, jnp.zeros((1, width), jnp.bfloat16)], axis=0)
    send_x = jnp.take(x_pad, source, axis=0).reshape(experts, capacity, width)
    recv_x, recv_live = (
        lax.all_to_all(send_x, "expert", split_axis=0, concat_axis=0, tiled=True),
        lax.all_to_all(
            occupied.reshape(experts, capacity), "expert", split_axis=0, concat_axis=0, tiled=True
        ),
    )
    x_rows = recv_x.reshape(-1, width)
    parts = (x_rows,)
    part_gate = jnp.dot(parts[0], wg, preferred_element_type=jnp.float32)
    part_up = jnp.dot(parts[0], wu, preferred_element_type=jnp.float32)
    pre_gate, pre_up = lax.psum((part_gate, part_up), "dp")
    sig = jax.nn.sigmoid(pre_gate)
    silu_v = pre_gate * sig
    acted = (silu_v * pre_up).astype(jnp.bfloat16)
    cf = cotangent[0].astype(jnp.float32)
    gate_part = (cf * pre_up * sig * (1.0 + pre_gate * (1.0 - sig))).astype(jnp.bfloat16)
    up_part = (cf * silu_v).astype(jnp.bfloat16)
    contract = (((0,), (0,)), ((), ()))
    gate_grad = lax.dot_general(x_rows, gate_part, contract, preferred_element_type=jnp.float32)
    up_grad = lax.dot_general(x_rows, up_part, contract, preferred_element_type=jnp.float32)
    parts = (gate_part, up_part)
    back = lax.dot_general(
        parts[0], wg, (((1,), (1,)), ((), ())), preferred_element_type=jnp.float32
    ) + lax.dot_general(parts[1], wu, (((1,), (1,)), ((), ())), preferred_element_type=jnp.float32)
    back = (back,)[0]
    whole = lax.psum(back, "section")
    home = lax.all_to_all(
        whole.reshape(experts, capacity, width), "expert", split_axis=0, concat_axis=0, tiled=True
    )
    token_grad = jnp.sum(
        jnp.take(home.reshape(-1, width), slot, axis=0).reshape(rows, 2, width), axis=1
    )
    return (
        acted[None],
        token_grad.astype(jnp.bfloat16),
        gate_grad.astype(jnp.bfloat16)[None],
        up_grad.astype(jnp.bfloat16)[None],
    )


def solution(mesh):
    placed = (
        P("expert", "dp"),
        P("expert", None),
        P("expert", "dp", "section"),
        P("expert", "dp", "section"),
        P("expert", None, "section"),
    )
    return jax.shard_map(
        local,
        mesh=mesh,
        in_specs=placed,
        out_specs=(
            P("expert", None, "section"),
            P("expert", "dp"),
            P("expert", "dp", "section"),
            P("expert", "dp", "section"),
        ),
        check_vma=False,
    )
```

profile of v0, /device:TPU:1, one launch (start us, length us, event | category | flops | bytes accessed | tf_op | source)
XLA Modules:
  0.0 297.3 jit_solution(851770255115678732)
XLA Ops:
  7.2 0.7 broadcast_multiply_fusion
  8.0 0.8 copy.14
  8.8 0.1 eq.29
  8.9 0.1 eq.25
  9.0 0.1 copy.13
  9.2 0.1 mul.45
  9.3 0.6 reduce-window.6
  9.9 0.2 slice_reduce_fusion
  10.3 1.4 scatter_custom_fusion
  11.8 0.9 concatenate.3
  12.7 2.0 gather_fusion
  14.8 0.1 broadcast_select_fusion
  14.9 21.5 %all_to_all.10 = bf16[8,64,768]{2,1,0:T(8,128)(2,1)S(1)} all-to-all(bf16[8,64,768]{2,1,0:T(8,128)(2,1)S(1)} %broadcast_select_fusion), channel_id=1, replica_groups=mesh['section'=16,'expert'=8,'dp'=4] {'expert'}, dimensions={0} | all-to-all | bytes 1572864 | tf_op jit(solution)/shard_map/all_to_all | solution.py:23
  36.4 1.6 fusion.8
  38.1 1.6 fusion.12
  39.7 73.3 %all-reduce.7.cloned.1.call-done = (f32[512,512]{1,0:T(8,128)}, f32[512,512]{1,0:T(8,128)}) async-done(((f32[512,512]{1,0:T(8,128)}, f32[512,512]{1,0:T(8,128)}), (f32[512,512]{1,0:T(8,128)}, f32[512,512]{1,0:T(8,128)})) %all-reduce.7.cloned.1.call-update) | async-done | bytes 2097168 | tf_op jit(solution)/shard_map/psum | solution.py:32
  113.0 2.9 fusion.4
  115.9 0.6 fusion.10
  116.5 0.8 copy-done.2
  117.3 0.2 copy-done.5
  117.5 0.1 copy-done.7
  117.7 1.9 convolution_add_fusion
  119.7 132.2 %all-reduce.5.cloned.1.call-done = f32[8,64,768]{2,1,0:T(8,128)} async-done(((f32[8,64,768]{2,1,0:T(8,128)}), f32[8,64,768]{2,1,0:T(8,128)}) %all-reduce.5.cloned.1.call-update) | async-done | bytes 1572880 | tf_op jit(solution)/shard_map/psum | solution.py:47
  251.8 14.7 %all-to-all-start.1 = ((f32[8,64,768]{2,1,0:T(8,128)}), f32[8,64,768]{2,1,0:T(8,128)S(1)}, u32[]{:S(2)}, u32[]{:S(2)}) async-start(f32[8,64,768]{2,1,0:T(8,128)} %all-reduce.5.cloned.1.call-done), calls=%async_computation.1 | async-start | bytes 3145728 | tf_op jit(solution)/shard_map/all_to_all | solution.py:48
  266.5 0.1 reduce_sum.24
  266.7 0.1 copy.17
  266.9 2.6 fusion
  269.6 1.6 fusion.1
  271.2 15.9 %all-to-all-done.1 = f32[8,64,768]{2,1,0:T(8,128)S(1)} async-done(((f32[8,64,768]{2,1,0:T(8,128)}), f32[8,64,768]{2,1,0:T(8,128)S(1)}, u32[]{:S(2)}, u32[]{:S(2)}) %all-to-all-start.1) | async-done | bytes 1572896 | tf_op jit(solution)/shard_map/all_to_all | solution.py:48
  287.1 1.1 gather_fusion.1
  288.2 0.5 gather.15
  288.7 1.8 select_reduce_fusion
  (34 shorter events, 0.5 us)
Async XLA Ops:
  7.2 30.9 %copy-start = (bf16[1,768,512]{2,1,0:T(8,128)(2,1)S(1)}, bf16[1,768,512]{2,1,0:T(8,128)(2,1)}, u32[]{:S(2)}) copy-start(bf16[1,768,512]{2,1,0:T(8,128)(2,1)} %param.7) | copy-start | bytes 2359300
  7.2 105.8 %all-reduce.7.cloned.1.call-start = ((), (), s32[]{:S(2)}) async-start(), calls=%async_computation.3 | async-start | bytes 4194304 | tf_op jit(solution)/shard_map/psum | solution.py:32
  14.8 21.7 %copy-start.4 = (bf16[1,768,512]{2,1,0:T(8,128)(2,1)S(1)}, bf16[1,768,512]{2,1,0:T(8,128)(2,1)}, u32[]{:S(2)}) copy-start(bf16[1,768,512]{2,1,0:T(8,128)(2,1)} %param.8) | copy-start | bytes 2359300
  39.6 73.4 %copy-start.6 = (bf16[1,512,512]{2,1,0:T(8,128)(2,1)S(1)}, bf16[1,512,512]{2,1,0:T(8,128)(2,1)}, u32[]{:S(2)}) copy-start(bf16[1,512,512]{2,1,0:T(8,128)(2,1)} %param.9) | copy-start | bytes 1572868
  39.6 212.2 %all-reduce.5.cloned.1.call-start = ((), (), s32[]{:S(2)}) async-start(), calls=%async_computation.2 | async-start | bytes 3145728 | tf_op jit(solution)/shard_map/psum | solution.py:47
  115.9 3.7 %copy-start.1 = (bf16[512,512]{1,0:T(8,128)(2,1)}, bf16[512,512]{1,0:T(8,128)(2,1)S(1)}, u32[]{:S(2)}) copy-start(bf16[512,512]{1,0:T(8,128)(2,1)S(1)} %get-tuple-element.6) | copy-start | bytes 1572868
  115.9 1.4 copy-start.2
  115.9 1.6 copy-start.5
  115.9 1.8 copy-start.7
  119.6 147.1 %copy-start.9 = (s32[128,2]{0,1:T(2,128)S(1)}, s32[128,2]{0,1:T(2,128)}, u32[]{:S(2)}) copy-start(s32[128,2]{0,1:T(2,128)} %param.6) | copy-start | bytes 3076
  251.8 35.3 %all-to-all-start.1 = ((f32[8,64,768]{2,1,0:T(8,128)}), f32[8,64,768]{2,1,0:T(8,128)S(1)}, u32[]{:S(2)}, u32[]{:S(2)}) async-start(f32[8,64,768]{2,1,0:T(8,128)} %all-reduce.5.cloned.1.call-done), calls=%async_computation.1 | async-start | bytes 3145728 | tf_op jit(solution)/shard_map/all_to_all | solution.py:48
  266.9 2.7 copy-start.3
  266.9 2.7 copy-start.8
Sparse Core Ops, SparseCore 0:
  39.8 73.2 all-reduce.6
  119.8 132.0 all-reduce.4
where the time goes:
time: 298 us; the launch traced here: 297 us
  waiting for transfers between devices  221 us (74%)
  blocking collectives  21.5 us (7%)
  starting transfers between devices  14.8 us (5%)
  between operations  14.2 us (5%)
  matrix products  9.94 us (3%)
  local copies, waits for them, and re-layouts  9.07 us (3%)
  other arithmetic  6.29 us (2%)
    psum x1, waiting for transfers between devices, local(): whole = lax.psum(back, 'section')  132 us
    psum x1, waiting for transfers between devices, local(): pre_gate, pre_up = lax.psum((part_gate, part_up), 'dp')  73.3 us
    all_to_all x1, blocking collectives, local(): lax.all_to_all(send_x, 'expert', split_axis=0, concat_axis=0, tiled=True)  21.5 us
    all_to_all x1, waiting for transfers between devices, local(): lax.all_to_all(whole.reshape(experts, capacity, width), 'expert', split_a...  15.9 us
    all_to_all x1, starting transfers between devices, local(): lax.all_to_all(whole.reshape(experts, capacity, width), 'expert', split_a...  14.7 us
  transfers between devices with their start and end apart: 3, of which 3 were waited for; matrix products, arithmetic and copies ran while one was open for 2% of the time, Pallas kernels for 0%

commit v1 on v0

--- a/solution.py
+++ b/solution.py
@@ -44,7 +44,7 @@
         parts[0], wg, (((1,), (1,)), ((), ())), preferred_element_type=jnp.float32
     ) + lax.dot_general(parts[1], wu, (((1,), (1,)), ((), ())), preferred_element_type=jnp.float32)
     back = (back,)[0]
-    whole = lax.psum(back, "section")
+    whole = jnp.sum(lax.all_gather(back, "section"), axis=0)
     home = lax.all_to_all(
         whole.reshape(experts, capacity, width), "expert", split_axis=0, concat_axis=0, tiled=True
     )

time: 298 us -> 443 us (1.49)
  waiting for transfers between devices: 221 us -> 364 us
  other arithmetic: 6.29 us -> 17 us
  starting transfers between devices: 14.8 us -> 5.34 us
    all_gather x0 -> x1, waiting for transfers between devices: none -> 274 us  [local(): whole = jnp.sum(lax.all_gather(back, 'section'), axis=0)]
    psum x1 -> x0, waiting for transfers between devices: 132 us -> none  [local(): whole = lax.psum(back, 'section')]
    reduce_sum x0 -> x1, other arithmetic: none -> 10.7 us  [local(): whole = jnp.sum(lax.all_gather(back, 'section'), axis=0)]
    all_to_all x1, starting transfers between devices: 14.7 us -> 5.26 us  [local(): lax.all_to_all(whole.reshape(experts, capacity, width), 'expert', split_a...]
  transfers between devices with their start and end apart: 3 -> 3, of which waited for: 3 -> 3; matrix products, arithmetic and copies ran while one was open for 2% -> 1% of each run, Pallas kernels for 0% -> 0%
where the time goes in v1:
time: 443 us; the launch traced here: 442 us
  waiting for transfers between devices  364 us (82%)
  blocking collectives  21.5 us (5%)
  other arithmetic  17 us (4%)
  between operations  14.2 us (3%)
  local copies, waits for them, and re-layouts  10.7 us (2%)
  matrix products  10 us (2%)
  starting transfers between devices  5.34 us (1%)
    all_gather x1, waiting for transfers between devices, local(): whole = jnp.sum(lax.all_gather(back, 'section'), axis=0)  274 us
    psum x1, waiting for transfers between devices, local(): pre_gate, pre_up = lax.psum((part_gate, part_up), 'dp')  73.3 us
    all_to_all x1, blocking collectives, local(): lax.all_to_all(send_x, 'expert', split_axis=0, concat_axis=0, tiled=True)  21.5 us
    all_to_all x1, waiting for transfers between devices, local(): lax.all_to_all(whole.reshape(experts, capacity, width), 'expert', split_a...  15.9 us
    reduce_sum x1, other arithmetic, local(): whole = jnp.sum(lax.all_gather(back, 'section'), axis=0)  10.7 us
  transfers between devices with their start and end apart: 3, of which 3 were waited for; matrix products, arithmetic and copies ran while one was open for 1% of the time, Pallas kernels for 0%

profile of v1, /device:TPU:1, one launch (start us, length us, event | category | flops | bytes accessed | tf_op | source)
XLA Modules:
  0.0 442.5 jit_solution(3256196006250622005)
XLA Ops:
  7.2 0.7 broadcast_multiply_fusion
  8.0 0.8 copy.14
  8.8 0.1 eq.29
  8.9 0.1 eq.25
  9.0 0.1 copy.13
  9.2 0.1 mul.45
  9.3 0.6 reduce-window.6
  9.9 0.2 slice_reduce_fusion
  10.2 0.1 fusion.16
  10.3 1.4 scatter_custom_fusion
  11.8 0.9 concatenate.3
  12.7 2.0 gather_fusion
  14.8 0.1 broadcast_select_fusion
  14.9 21.5 %all_to_all.10 = bf16[8,64,768]{2,1,0:T(8,128)(2,1)S(1)} all-to-all(bf16[8,64,768]{2,1,0:T(8,128)(2,1)S(1)} %broadcast_select_fusion), channel_id=1, replica_groups=mesh['section'=16,'expert'=8,'dp'=4] {'expert'}, dimensions={0} | all-to-all | bytes 1572864 | tf_op jit(solution)/shard_map/all_to_all | solution.py:23
  36.4 1.6 fusion.8
  38.1 1.6 fusion.12
  39.7 73.3 %all-reduce.4.cloned.1.call-done = (f32[512,512]{1,0:T(8,128)}, f32[512,512]{1,0:T(8,128)}) async-done(((f32[512,512]{1,0:T(8,128)}, f32[512,512]{1,0:T(8,128)}), (f32[512,512]{1,0:T(8,128)}, f32[512,512]{1,0:T(8,128)})) %all-reduce.4.cloned.1.call-update) | async-done | bytes 2097168 | tf_op jit(solution)/shard_map/psum | solution.py:32
  113.0 2.9 fusion.4
  115.9 0.8 copy-done.1
  116.7 0.6 fusion.10
  117.3 2.0 convolution_add_fusion
  119.4 274.4 %all-gather.3.cloned.1.call-done = f32[8192,768]{1,0:T(8,128)} async-done(((f32[512,768]{1,0:T(8,128)}), f32[8192,768]{1,0:T(8,128)}) %all-gather.3.cloned.1.call-update) | async-done | bytes 25165840 | tf_op jit(solution)/shard_map/all_gather | solution.py:47
  393.8 10.7 %reduce_sum.34 = f32[512,768]{1,0:T(8,128)} reduce(f32[16,512,768]{2,1,0:T(8,128)} %bitcast.45, f32[]{:T(128)} %constant.60.clone.1), dimensions={0}, to_apply=%region_6.7 | reduce | flops 5898240 | bytes 26738692 | tf_op jit(solution)/shard_map/reduce_sum | solution.py:47
  404.5 5.3 %all-to-all-start.1 = ((f32[8,64,768]{2,1,0:T(8,128)}), f32[8,64,768]{2,1,0:T(8,128)S(1)}, u32[]{:S(2)}, u32[]{:S(2)}) async-start(f32[8,64,768]{2,1,0:T(8,128)} %bitcast.50), calls=%async_computation.1 | async-start | bytes 3145728 | tf_op jit(solution)/shard_map/all_to_all | solution.py:48
  409.7 0.1 reduce_sum.33
  410.0 0.1 copy.17
  410.2 2.6 fusion
  412.8 1.6 fusion.1
  414.4 15.9 %all-to-all-done.1 = f32[8,64,768]{2,1,0:T(8,128)S(1)} async-done(((f32[8,64,768]{2,1,0:T(8,128)}), f32[8,64,768]{2,1,0:T(8,128)S(1)}, u32[]{:S(2)}, u32[]{:S(2)}) %all-to-all-start.1) | async-done | bytes 1572896 | tf_op jit(solution)/shard_map/all_to_all | solution.py:48
  430.3 2.0 gather_fusion.1
  432.3 1.6 gather.15
  433.9 1.8 select_reduce_fusion
  (31 shorter events, 0.4 us)
Async XLA Ops:
  7.2 30.9 %copy-start = (bf16[1,768,512]{2,1,0:T(8,128)(2,1)S(1)}, bf16[1,768,512]{2,1,0:T(8,128)(2,1)}, u32[]{:S(2)}) copy-start(bf16[1,768,512]{2,1,0:T(8,128)(2,1)} %param.7) | copy-start | bytes 2359300
  7.2 105.8 %all-reduce.4.cloned.1.call-start = ((), (), s32[]{:S(2)}) async-start(), calls=%async_computation.3 | async-start | bytes 4194304 | tf_op jit(solution)/shard_map/psum | solution.py:32
  14.8 21.7 %copy-start.4 = (bf16[1,768,512]{2,1,0:T(8,128)(2,1)S(1)}, bf16[1,768,512]{2,1,0:T(8,128)(2,1)}, u32[]{:S(2)}) copy-start(bf16[1,768,512]{2,1,0:T(8,128)(2,1)} %param.8) | copy-start | bytes 2359300
  39.6 73.4 %copy-start.5 = (bf16[1,512,512]{2,1,0:T(8,128)(2,1)S(1)}, bf16[1,512,512]{2,1,0:T(8,128)(2,1)}, u32[]{:S(2)}) copy-start(bf16[1,512,512]{2,1,0:T(8,128)(2,1)} %param.9) | copy-start | bytes 1572868
  39.6 354.2 %all-gather.3.cloned.1.call-start = ((), (), s32[]{:S(2)}) async-start(), calls=%async_computation.2 | async-start | bytes 26738688 | tf_op jit(solution)/shard_map/all_gather | solution.py:47
  115.9 0.8 copy-start.1
  115.9 1.4 copy-start.2
  404.5 5.5 %copy-start.7 = (s32[128,2]{0,1:T(2,128)S(1)}, s32[128,2]{0,1:T(2,128)}, u32[]{:S(2)}) copy-start(s32[128,2]{0,1:T(2,128)} %param.6) | copy-start | bytes 3076
  404.5 25.8 %all-to-all-start.1 = ((f32[8,64,768]{2,1,0:T(8,128)}), f32[8,64,768]{2,1,0:T(8,128)S(1)}, u32[]{:S(2)}, u32[]{:S(2)}) async-start(f32[8,64,768]{2,1,0:T(8,128)} %bitcast.50), calls=%async_computation.1 | async-start | bytes 3145728 | tf_op jit(solution)/shard_map/all_to_all | solution.py:48
  410.1 2.7 copy-start.3
  410.1 2.7 copy-start.6
Sparse Core Ops, SparseCore 0:
  39.8 73.2 all-reduce.3
  119.5 274.2 all-gather.2
